TPU v7x, 256 devices: a whole 4x4x8 slice. The times are simulated.
256 devices in a mesh: seq: 32 (over y, z), head: 4 (over x), dp: 2 (over core).
Axes of the slice: x: 4, y: 4, z: 8, core: 2. Of those that a mesh axis runs over, the one named last changes fastest.
Arguments:
- inputs: bfloat16 [2, 16384, 3584], P('dp', 'seq', 'head'), may hold values from -6 to 6
- value_weight: bfloat16 [3584, 3584], P(None, 'head'), may hold values from -0.09375 to 0.09375
- cotangent: bfloat16 [2, 16384, 3584], P('dp', 'seq', 'head'), may hold values from -6 to 6
- spikes_q: int32 [2, 16384, 3584], P('dp', 'seq', 'head'), may hold values from 0 to 3
- spikes_k: int32 [2, 16384, 3584], P('dp', 'seq', 'head'), may hold values from 0 to 3
- log_decay: float32 [2, 28, 16384], P('dp', 'head', 'seq'), may hold values from -1.0976562 to 0, as said below
Outputs:
- grad_input: bfloat16 [2, 16384, 3584], P('dp', 'seq', 'head')
- grad_weight: float32 [3584, 3584], P(('seq', 'dp'), 'head')
Inputs may be any that keep to these rules, and one draw needn't show every extreme that they name: `spikes_q`: spike count of a token in a channel. `spikes_k`: spike count of a token in a channel. `log_decay`: negative.
All inputs are finite; a program needn't handle non-finite values.
Results may differ from a plain program's by a relative error of at most 0.0051.
Values may be sent and summed in bfloat16 or wider, within the bound.
A program may use at most 128 MiB of HBM per device.

v0:
```python
import math

import jax
import jax.numpy as jnp
from jax import lax
from jax.sharding import PartitionSpec as P


def carried_in(array, axis, combine, identity):
    count, mine = (lax.axis_size(axis), lax.axis_index(axis))
    everything = jax.tree.map(lambda part: lax.all_gather(part, axis), array)
    start = jax.tree.map(
        lambda part, zero: jnp.broadcast_to(jnp.asarray(zero, part.dtype), part.shape),
        array,
        identity,
    )

    def lap(k, before):
        at = count - 1 - k
        reached = at > mine
        new = combine(before, jax.tree.map(lambda part: part[at], everything))
        return jax.tree.map(lambda a, b: jnp.where(reached, a, b), new, before)

    return lax.fori_loop(0, count, lap, start)


def chain_step(earlier, later_part):
    return (later_part[0] * earlier[0], later_part[1] + later_part[0][:, None, None] * earlier[1])


def local(inputs, value_weight, cotangent, spikes_q, spikes_k, log_decay):
    token_count = inputs.shape[1]
    feature_count = value_weight.shape[1]
    heads_here = log_decay.shape[1]
    head_size = feature_count // heads_here
    block_rows = min(token_count, 512)
    block_count = token_count // block_rows
    seq_length = token_count * lax.axis_size("seq")
    grad_scale = 1.0 / (2.25 * head_size * math.sqrt(seq_length))
    shape_four = (block_count, block_rows, heads_here, head_size)
    query_bf = spikes_q.reshape(shape_four).astype(jnp.bfloat16)
    query_f32 = spikes_q.reshape(shape_four).astype(jnp.float32)
    key_bf = spikes_k.reshape(shape_four).astype(jnp.bfloat16)
    key_f32 = spikes_k.reshape(shape_four).astype(jnp.float32)
    grads_out = cotangent.reshape(shape_four)
    cumulative = jnp.cumsum(log_decay.reshape(heads_here, block_count, block_rows), axis=2)
    scores = jnp.einsum("nthd,nshd->hnts", query_bf, key_bf, preferred_element_type=jnp.float32)
    causal = jnp.arange(block_rows)[:, None] >= jnp.arange(block_rows)[None, :]
    log_gaps = jnp.where(causal, cumulative[..., :, None] - cumulative[..., None, :], -jnp.inf)
    weighted = (scores * jnp.exp(log_gaps)).astype(jnp.bfloat16)
    local_part = jnp.einsum(
        "hnts,nthe->hnse", weighted, grads_out, preferred_element_type=jnp.float32
    )
    query_decayed = query_f32 * jnp.exp(cumulative).transpose(1, 2, 0)[..., None]
    state_terms = jnp.einsum(
        "nthd,nthe->hnde",
        query_decayed,
        grads_out.astype(jnp.float32),
        precision=lax.Precision.HIGHEST,
    )
    decays = jnp.exp(cumulative[..., -1])
    total_decay = decays[:, block_count - 1]
    total_term = state_terms[:, block_count - 1]
    identity = (jnp.ones_like(total_decay), jnp.zeros_like(total_term))
    carry_in = carried_in((total_decay, total_term), "seq", chain_step, identity)[1]
    block_states = [carry_in]
    states = jnp.stack(block_states, axis=1)
    carried = jnp.exp(cumulative[..., -1:] - cumulative)[..., None] * jnp.einsum(
        "nshd,hnde->hnse", key_f32, states, precision=lax.Precision.HIGHEST
    )
    value_grad = (grad_scale * (local_part + carried)).astype(jnp.bfloat16)
    value_grad = value_grad.transpose(1, 2, 0, 3).reshape(token_count, feature_count)
    all_features = lax.all_gather(inputs, "head", axis=2, tiled=True)[0]
    weight_part = lax.psum_scatter(
        lax.dot_general(
            all_features, value_grad, (((0,), (0,)), ((), ())), preferred_element_type=jnp.float32
        ),
        ("seq", "dp"),
        scatter_dimension=0,
        tiled=True,
    )
    grad_weight = weight_part * (1.0 / math.sqrt(lax.axis_size("dp") * seq_length))
    input_term = lax.dot_general(
        value_grad, value_weight, (((1,), (1,)), ((), ())), preferred_element_type=jnp.float32
    )
    grad_input = lax.psum_scatter(input_term, "head", scatter_dimension=1, tiled=True).astype(
        jnp.bfloat16
    )
    return (grad_input.reshape(1, token_count, -1), grad_weight)


def solution(mesh):
    return jax.shard_map(
        local,
        mesh=mesh,
        in_specs=(
            P("dp", "seq", "head"),
            P(None, "head"),
            P("dp", "seq", "head"),
            P("dp", "seq", "head"),
            P("dp", "seq", "head"),
            P("dp", "head", "seq"),
        ),
        out_specs=(P("dp", "seq", "head"), P(("seq", "dp"), "head")),
        check_vma=False,
    )
```

profile of v0, /device:TPU:5, one launch (start us, length us, event | category | flops | bytes accessed | tf_op | source)
XLA Modules:
  0.0 507.7 jit_solution(16697725110773820423)
XLA Ops:
  7.2 3.9 reduce-window.6
  11.6 2.8 copy.45
  14.4 3.5 fusion.16
  17.9 1.5 copy.52
  19.3 1.8 fusion.11
  24.4 64.4 %all-reduce = f32[224]{0:T(256)S(1)} all-reduce(f32[224]{0:T(256)S(1)} %dynamic-update-slice), channel_id=3, replica_groups=mesh['seq'=32,'head'=4,'dp'=2] {'seq'}, use_global_device_ids=true, to_apply=%add | all-reduce | flops 224 | bytes 1792
  89.0 1.8 copy.46
  90.8 1.9 fusion.15
  92.8 5.7 %fusion.1 = f32[7,512,128]{1,2,0:T(8,128)} fusion(bf16[512,7,128]{0,2,1:T(8,128)(2,1)S(1)} %bitcast.73, f32[7,512]{1,0:T(8,128)S(1)} %get-tuple-element.174, pred[512,512]{1,0:T(8,128)(4,1)S(1)} %iota_compare_fusion, bf16[512,7,128]{0,2,1:T(8,128)(2,1)} %bitcast.76, bf16[512,7,128]{0,2,1:T(8,128)(2,1)} %bitcast.77), kind=kOutput, calls=%fused_computation.5 | convolution fusion | flops 946864128 | bytes 4864000 | tf_op jit(solution)/shard_map/hnts,nthe->hnse/dot_general | solution.py:51
  98.4 54.8 %all-gather.7.cloned.1.call-done = f32[224,128,128]{2,1,0:T(8,128)} async-done(((f32[7,128,128]{2,1,0:T(8,128)}), f32[224,128,128]{2,1,0:T(8,128)}) %all-gather.7.cloned.1.call-update) | async-done | bytes 14680080 | tf_op jit(solution)/shard_map/all_gather | solution.py:11
  153.2 38.4 %while.16 = (s32[]{:T(128)}, f32[7,128,128]{2,1,0:T(8,128)S(1)}, s32[]{:T(128)}, f32[32,7,128,128]{3,2,1,0:T(8,128)}, f32[32,7]{1,0:T(8,128)S(1)}, /*index=5*/s32[]{:T(128)}, s32[]{:T(128)}, s32[]{:T(128)}, s32[]{:T(128)}) while((s32[]{:T(128)}, f32[7,128,128]{2,1,0:T(8,128)S(1)}, s32[]{:T(128)}, f32[32,7,128,128]{3,2,1,0:T(8,128)}, ...), condition=%wide.region_3.4_spmd.clone, body=%wide.region_2.3_spmd.clone.sunk | while | flops 458760 | bytes 1376507 | solution.py:24
  154.4 1.1 fusion.28
  155.6 1.1 fusion.28
  156.8 1.1 fusion.28
  158.0 1.1 fusion.28
  159.2 1.1 fusion.28
  160.4 1.1 fusion.28
  161.6 1.1 fusion.28
  164.0 1.2 fusion.28
  165.2 1.2 fusion.28
  166.5 1.2 fusion.28
  167.7 1.2 fusion.28
  168.9 1.1 fusion.28
  170.1 1.1 fusion.28
  171.3 1.1 fusion.28
  172.5 1.1 fusion.28
  173.7 1.1 fusion.28
  174.9 1.1 fusion.28
  176.1 1.1 fusion.28
  177.3 1.2 fusion.28
  178.5 1.1 fusion.28
  180.9 1.1 fusion.28
  182.1 1.1 fusion.28
  183.3 1.1 fusion.28
  184.5 1.1 fusion.28
  185.7 1.1 fusion.28
  186.9 1.1 fusion.28
  188.1 1.1 fusion.28
  189.3 1.1 fusion.28
  190.5 1.1 fusion.28
  191.6 3.3 fusion.10
  195.0 3.1 all-gather.5.cloned.1.call-done
  198.1 8.5 %convolution_bitcast_fusion = f32[3584,896]{0,1:T(8,128)} fusion(bf16[512,896]{0,1:T(8,128)(2,1)S(1)} %bitcast.74, bf16[1,512,3584]{2,1,0:T(8,128)(2,1)} %all-gather.5.cloned.1.call-done), kind=kOutput, calls=%fused_computation.3 | convolution fusion | flops 3288334336 | bytes 17432576 | tf_op jit(solution)/shard_map/dot_general | solution.py:75
  206.8 8.9 %fusion.17 = f32[512,3584]{1,0:T(8,128)} fusion(bf16[512,896]{0,1:T(8,128)(2,1)S(1)} %bitcast.75, bf16[3584,896]{1,0:T(8,128)(2,1)} %param.9), kind=kOutput, calls=%fused_computation.32 | convolution fusion | flops 3288334336 | bytes 14680064 | tf_op jit(solution)/shard_map/dot_general | solution.py:83
  217.7 205.1 %all-reduce.4.cloned.1.call-done = f32[3584,896]{0,1:T(8,128)} async-done(((f32[3584,896]{0,1:T(8,128)}), f32[3584,896]{0,1:T(8,128)}) %all-reduce.4.cloned.1.call-update) | async-done | bytes 12845072
  422.8 1.4 dynamic-slice_multiply_fusion
  425.0 73.6 %reduce-scatter.3.cloned.1.call-done = f32[512,896]{1,0:T(8,128)} async-done(((f32[512,3584]{1,0:T(8,128)}), f32[512,896]{1,0:T(8,128)}) %reduce-scatter.3.cloned.1.call-update) | async-done | bytes 1835024 | tf_op jit(solution)/shard_map/reduce_scatter | solution.py:86
  498.7 2.5 convert_bitcast_fusion
  (70 shorter events, 9.3 us)
Async XLA Ops:
  7.2 146.0 %all-gather.7.cloned.1.call-start = ((), (), s32[]{:S(2)}) async-start(), calls=%async_computation.3 | async-start | bytes 15138816 | tf_op jit(solution)/shard_map/all_gather | solution.py:11
  19.3 3.6 copy-start.3
  21.2 176.9 %all-gather.5.cloned.1.call-start = ((), (), s32[]{:S(2)}) async-start(), calls=%async_computation.2 | async-start | bytes 4587520 | tf_op jit(solution)/shard_map/all_gather | solution.py:73
  21.9 400.9 %all-reduce.4.cloned.1.call-start = ((), (), s32[]{:S(2)}) async-start(), calls=%async_computation.4 | async-start | bytes 25690112
  90.8 1.9 copy-start.1
  92.7 98.9 %copy-start = (f32[1,512,896]{1,2,0:T(8,128)S(1)}, f32[1,512,896]{1,2,0:T(8,128)}, u32[]{:S(2)}) copy-start(f32[1,512,896]{1,2,0:T(8,128)} %get-tuple-element.177) | copy-start | bytes 5505028
  206.6 292.1 %reduce-scatter.3.cloned.1.call-start = ((), (), s32[]{:S(2)}) async-start(), calls=%async_computation.1 | async-start | bytes 9175040 | tf_op jit(solution)/shard_map/reduce_scatter | solution.py:86
  215.8 0.7 copy-start.2
Sparse Core Ops, SparseCore 0:
  21.3 131.8 all-gather.6
  155.0 42.9 all-gather.4
  206.7 216.0 all-reduce.3
  425.2 73.4 reduce-scatter.2
where the time goes:
time: 512 us; the launch traced here: 508 us
  waiting for transfers between devices  337 us (66%)
  blocking collectives  64.4 us (13%)
  other arithmetic  50.1 us (10%)
  matrix products  28.2 us (6%)
  between operations  15.2 us (3%)
  local copies, waits for them, and re-layouts  10.6 us (2%)
    unnamed x5, waiting for transfers between devices  206 us
    reduce_scatter x1, waiting for transfers between devices, local(): lax.psum_scatter(input_term, 'head', scatter_dimension=1, tiled=True)  73.6 us
    unnamed x1, blocking collectives  64.4 us
    all_gather x1, waiting for transfers between devices, carried_in(): everything = jax.tree.map(lambda part: lax.all_gather(part, axis), array)  54.8 us
    select_n x32, other arithmetic, lap(): return jax.tree.map(lambda a, b: jnp.where(reached, a, b), new, before)  36.8 us
  transfers between devices with their start and end apart: 4, of which 4 were waited for; matrix products, arithmetic and copies ran while one was open for 12% of the time, Pallas kernels for 0%

commit v1 on v0

v1 whole, which is shorter than its diff:
```python
import math

import jax
import jax.numpy as jnp
from jax import lax
from jax.experimental import pallas as pl
from jax.experimental.pallas import tpu as pltpu
from jax.sharding import PartitionSpec as P

NX, NY, NZ = 4, 4, 8
T, F, H, E = 512, 896, 7, 128
HT = T // 2
HF = F // 2
ZR = F // NZ
OUT = ZR // 2
SL = E // NZ
YROWS = H * SL + 8
CUTS = ((0, 512), (512, 384))
BF, F32 = jnp.bfloat16, jnp.float32
MESH = pl.DeviceIdType.MESH

_names = {}
_count = 0
for _name, _n in (
    ("dz", 8), ("a1", 8), ("a2", 8), ("yx", 4), ("xd", 2), ("xp", 1), ("xf", 2), ("vg", 1),
    ("xh", 2), ("xs", 4), ("yh", 2), ("ys", 4), ("zp", 8), ("zm", 6), ("fp", 1),
):
    _names[_name] = _count
    _count += _n
NSEM = _count


def dot(a, b, ca, cb):
    return lax.dot_general(a, b, (((ca,), (cb,)), ((), ())), preferred_element_type=F32)


def kernel(
    grad_scale, weight_scale,
    x_hbm, w_hbm, g_hbm, q_hbm, k_hbm, ld_ref,
    gi_hbm, gw_hbm,
    wv, gv, qv, kv, xg, cumr, cumc, dzs, dzr, tsend, trecv, lbuf, ysend, yrecv, csend, crecv,
    loc, vgs, p2s, pss, pf, xh, xf, gio, dwf, dsend, yh, yf, zps, zpr, zms, zmr, fin, gwv,
    ss, rs, ls,
):
    s = lax.axis_index("seq")
    x = lax.axis_index("head")
    c = lax.axis_index("dp")
    y, z = lax.div(s, NZ), lax.rem(s, NZ)
    half_x, par_x = lax.div(x, 2), lax.rem(x, 2)
    half_y, par_y = lax.div(y, 2), lax.rem(y, 2)
    other = 1 - c
    xp, xm = lax.rem(x + 1, NX), lax.rem(x + NX - 1, NX)
    yp, ym = lax.rem(y + 1, NY), lax.rem(y + NY - 1, NY)
    zp, zm = lax.rem(z + 1, NZ), lax.rem(z + NZ - 1, NZ)

    def dev(yy=None, zz=None, xx=None, cc=None):
        yy = y if yy is None else yy
        zz = z if zz is None else zz
        return (yy * NZ + zz, x if xx is None else xx, c if cc is None else cc)

    def rcopy(src, dst, name, send, recv, to):
        base = _names[name]
        return pltpu.make_async_remote_copy(
            src_ref=src, dst_ref=dst, send_sem=ss.at[base + send], recv_sem=rs.at[base + recv],
            device_id=to, device_id_type=MESH,
        )

    loads = [
        pltpu.make_async_copy(q_hbm.at[0], qv, ls.at[0]),
        pltpu.make_async_copy(g_hbm.at[0], gv, ls.at[1]),
        pltpu.make_async_copy(k_hbm.at[0], kv, ls.at[2]),
        pltpu.make_async_copy(w_hbm, wv, ls.at[3]),
    ]
    for load in loads:
        load.start()

    barrier = pltpu.get_barrier_semaphore()
    greet = [dev(xx=xp, cc=c), dev(xx=xp, cc=other), dev(xx=xm, cc=c), dev(xx=xm, cc=other), dev(cc=other)]
    greet += [dev(yy=lax.rem(y + k, NY)) for k in range(1, NY)]
    greet += [dev(zz=lax.rem(z + k, NZ)) for k in range(1, NZ)]
    for to in greet:
        pl.semaphore_signal(barrier, inc=1, device_id=to, device_id_type=MESH)
    pl.semaphore_wait(barrier, len(greet))

    x_own = c == half_x
    x_odd = 1 - par_x
    x_rel = lax.rem(2 * c + x_odd - x + NX, NX)
    mine = xg.at[par_x, c]
    to_p = rcopy(x_hbm.at[0], mine, "xd", 0, c, dev(xx=xp, cc=half_x))
    to_m = rcopy(x_hbm.at[0], mine, "xd", 1, c, dev(xx=xm, cc=half_x))
    to_p.start()
    to_m.start()
    own_in = pltpu.make_async_copy(x_hbm.at[0], mine, ls.at[4])
    to_other = rcopy(x_hbm.at[0], mine, "xp", 0, 0, dev(cc=other))

    @pl.when(x_own)
    def _():
        own_in.start()

    @pl.when(jnp.logical_not(x_own))
    def _():
        to_other.start()

    upper = (
        lax.broadcasted_iota(jnp.int32, (T, T), 0) <= lax.broadcasted_iota(jnp.int32, (T, T), 1)
    ).astype(F32).astype(BF)
    cumr[...] = jnp.zeros_like(cumr)
    cumr[0:H, :] = ld_ref[0]
    rest = cumr[...]
    total = jnp.zeros((E, T), F32)
    for _ in range(3):
        part = rest.astype(BF)
        total = total + dot(part, upper, 1, 0)
        rest = rest - part.astype(F32)
    cumr[...] = total
    cumc[...] = total.T
    dzs[...] = jnp.broadcast_to(cumr[0:8, T - 1 : T], (8, E))
    dzr[pl.ds(z, 1)] = dzs[...][None]
    sent_dz = []
    for k in range(1, NZ):
        copy = rcopy(dzs, dzr.at[z], "dz", k, k, dev(zz=lax.rem(z + k, NZ)))
        copy.start()
        sent_dz.append(copy)

    lane = lax.broadcasted_iota(jnp.int32, (T, E), 1)

    def column(h):
        return jnp.sum(jnp.where(lane == h, cumc[...], 0.0), axis=1, keepdims=True)

    def cols(h):
        return pl.ds(pl.multiple_of(h * E, E), E)

    loads[0].wait()
    loads[1].wait()

    def term_of(h, carry):
        scaled = gv[:, cols(h)].astype(F32) * jnp.exp(column(h))
        high = scaled.astype(BF)
        low = (scaled - high.astype(F32)).astype(BF)
        query = qv[:, cols(h)].astype(F32).astype(BF)
        term = dot(query, high, 0, 0) + dot(query, low, 0, 0)
        tsend[:, h] = term.astype(BF).reshape(NZ, SL, E)
        return carry

    lax.fori_loop(0, H, term_of, 0)
    trecv[pl.ds(z, 1)] = tsend[pl.ds(z, 1)]
    sent_a1 = []
    for k in range(1, NZ):
        to = lax.rem(z + k, NZ)
        copy = rcopy(tsend.at[to], trecv.at[z], "a1", k, k, dev(zz=to))
        copy.start()
        sent_a1.append(copy)

    loads[2].wait()

    def local_of(h, carry):
        query = qv[:, cols(h)].astype(F32).astype(BF)
        row = cumr[pl.ds(h, 1), :]
        col = column(h)
        for b in range(T // E):
            keys = kv[b * E : (b + 1) * E, cols(h)].astype(F32).astype(BF)
            width = T - b * E
            scores = dot(keys, query[b * E :, :], 1, 1)
            at = lax.broadcasted_iota(jnp.int32, (E, width), 0)
            tok = lax.broadcasted_iota(jnp.int32, (E, width), 1)
            gaps = jnp.where(tok >= at, row[:, b * E :] - col[b * E : (b + 1) * E, :], -jnp.inf)
            weighted = (scores * jnp.exp(gaps)).astype(BF)
            loc[b * E : (b + 1) * E, cols(h)] = dot(weighted, gv[b * E :, cols(h)], 1, 0)
        return carry

    lax.fori_loop(0, H, local_of, 0)

    for k in range(1, NZ):
        src = lax.rem(z + NZ - k, NZ)
        rcopy(dzs, dzr.at[src], "dz", k, k, dev()).wait_recv()
    for k in range(1, NZ):
        src = lax.rem(z + NZ - k, NZ)
        rcopy(tsend.at[0], trecv.at[src], "a1", k, k, dev()).wait_recv()
    logs = [dzr[i] for i in range(NZ)]
    decays = [jnp.exp(v) for v in logs]
    for h in range(H):
        state = jnp.zeros((SL, E), F32)
        for i in range(NZ - 1, -1, -1):
            lbuf[i, h] = state
            state = trecv[i, h].astype(F32) + decays[i][h : h + 1, :] * state
        ysend[h * SL : (h + 1) * SL, :] = state
    later = [jnp.zeros((8, E), F32)]
    for i in range(NZ - 1, -1, -1):
        later.append(later[-1] + logs[i])
    ysend[H * SL :, :] = later[NZ]
    yrecv[pl.ds(y, 1)] = ysend[...][None]
    sent_yx = []
    for k in range(1, NY):
        copy = rcopy(ysend, yrecv.at[y], "yx", k, k, dev(yy=lax.rem(y + k, NY)))
        copy.start()
        sent_yx.append(copy)
    for k in range(1, NY):
        src = lax.rem(y + NY - k, NY)
        rcopy(ysend, yrecv.at[src], "yx", k, k, dev()).wait_recv()
    y_decay = [jnp.exp(yrecv[j, H * SL :, :]) for j in range(NY)]
    z_decay = [jnp.exp(later[NZ - 1 - i]) for i in range(NZ)]
    for h in range(H):
        state = jnp.zeros((SL, E), F32)
        for j in range(NY - 1, 0, -1):
            new = yrecv[j, h * SL : (h + 1) * SL, :] + y_decay[j][h : h + 1, :] * state
            state = jnp.where(y < j, new, state)
        for i in range(NZ):
            csend[i, h] = (lbuf[i, h] + z_decay[i][h : h + 1, :] * state).astype(BF)
    crecv[pl.ds(z, 1)] = csend[pl.ds(z, 1)]
    sent_a2 = []
    for k in range(1, NZ):
        to = lax.rem(z + k, NZ)
        copy = rcopy(csend.at[to], crecv.at[z], "a2", k, k, dev(zz=to))
        copy.start()
        sent_a2.append(copy)

    for i in range(2):
        rcopy(x_hbm.at[0], xg.at[x_odd, i], "xd", 0, i, dev()).wait_recv()
    rows_a, rows_b = pl.ds(0, HT), pl.ds(HT, HT)
    half_a, half_b = xg.at[x_odd, :, rows_a, :], xg.at[x_odd, :, rows_b, :]
    pass_a = rcopy(half_a, half_a, "xf", 0, 0, dev(xx=xm))
    pass_b = rcopy(half_b, half_b, "xf", 1, 1, dev(xx=xp))

    @pl.when(x_rel == 1)
    def _():
        pass_a.start()

    @pl.when(x_rel == 3)
    def _():
        pass_b.start()

    for k in range(1, NZ):
        src = lax.rem(z + NZ - k, NZ)
        rcopy(csend.at[0], crecv.at[src], "a2", k, k, dev()).wait_recv()

    def value_of(h, carry):
        col = column(h)
        keys = kv[:, cols(h)].astype(F32).astype(BF)
        carried = jnp.exp(col[T - 1 : T, :] - col) * dot(keys, crecv[:, h].reshape(E, E), 1, 0)
        vgs[c, :, cols(h)] = (grad_scale * (loc[:, cols(h)] + carried)).astype(BF)
        return carry

    lax.fori_loop(0, H, value_of, 0)
    sent_vg = rcopy(vgs.at[c], vgs.at[c], "vg", 0, 0, dev(cc=other))
    sent_vg.start()

    loads[3].wait()

    def product(to):
        block = wv[pl.ds(pl.multiple_of(to * F, F), F), :]
        return dot(vgs[c], block, 1, 1)

    p2s[...] = product(lax.rem(x + 2, NX)).astype(BF)
    sent_x = [
        rcopy(p2s.at[rows_a], xh.at[0], "xh", 0, 0, dev(xx=xp)),
        rcopy(p2s.at[rows_b], xh.at[1], "xh", 1, 1, dev(xx=xm)),
    ]
    for copy in sent_x:
        copy.start()
    near = product(xp)
    pf[0] = near[:HT]
    pss[0, HT:, :] = near[HT:].astype(BF)
    copy = rcopy(pss.at[0, rows_b], xf.at[0, rows_b], "xs", 0, 0, dev(xx=xp))
    copy.start()
    sent_x.append(copy)
    near = product(xm)
    pf[1] = near[HT:]
    pss[1, :HT, :] = near[:HT].astype(BF)
    copy = rcopy(pss.at[1, rows_a], xf.at[1, rows_a], "xs", 1, 1, dev(xx=xm))
    copy.start()
    sent_x.append(copy)

    y_own = c == half_y
    y_odd = 1 - par_y
    y_rel = lax.rem(2 * c + y_odd - y + NY, NY)

    @pl.when(x_own)
    def _():
        own_in.wait()
        rcopy(x_hbm.at[0], xg.at[par_x, other], "xp", 0, 0, dev()).wait_recv()

    @pl.when(jnp.logical_not(x_own))
    def _():
        far_a, far_b = xg.at[par_x, :, rows_a, :], xg.at[par_x, :, rows_b, :]
        rcopy(far_a, far_a, "xf", 0, 0, dev()).wait_recv()
        rcopy(far_b, far_b, "xf", 1, 1, dev()).wait_recv()

    rcopy(vgs.at[other], vgs.at[other], "vg", 0, 0, dev()).wait_recv()

    def weight_of(i, carry):
        slot = lax.rem(par_y + jnp.where(y_own, 1, 0) + i, 2)
        dwf[slot] = dot(xg[slot].reshape(2 * T, F), vgs[...].reshape(2 * T, F), 0, 0)
        dsend[slot] = dwf[slot].astype(BF)
        first_a, first_b = pl.ds(0, HF), pl.ds(HF, HF)

        @pl.when(jnp.logical_and(slot == par_y, jnp.logical_not(y_own)))
        def _():
            rcopy(dsend.at[slot, first_a], yh, "yh", 0, 0, dev(yy=yp)).start()
            rcopy(dsend.at[slot, first_b], yh, "yh", 1, 0, dev(yy=ym)).start()

        @pl.when(jnp.logical_and(slot == y_odd, y_rel == 1))
        def _():
            rcopy(dsend.at[slot, first_b], yf.at[0, first_b], "ys", 1, 1, dev(yy=yp)).start()

        @pl.when(jnp.logical_and(slot == y_odd, y_rel == 3))
        def _():
            rcopy(dsend.at[slot, first_a], yf.at[1, first_a], "ys", 2, 2, dev(yy=ym)).start()

        return carry

    lax.fori_loop(0, 2, weight_of, 0)

    rcopy(p2s.at[rows_a], xh.at[0], "xh", 0, 0, dev()).wait_recv()
    pss[0, :HT, :] = (pf[0] + xh[0].astype(F32)).astype(BF)
    copy = rcopy(pss.at[0, rows_a], xf.at[0, rows_a], "xs", 2, 2, dev(xx=xp))
    copy.start()
    sent_x.append(copy)
    rcopy(p2s.at[rows_b], xh.at[1], "xh", 1, 1, dev()).wait_recv()
    pss[1, HT:, :] = (pf[1] + xh[1].astype(F32)).astype(BF)
    copy = rcopy(pss.at[1, rows_b], xf.at[1, rows_b], "xs", 3, 3, dev(xx=xm))
    copy.start()
    sent_x.append(copy)
    loc[...] = product(x)

    rows_a4, rows_b4 = pl.ds(0, HF), pl.ds(HF, HF)
    rcopy(dsend.at[0, rows_a4], yh, "yh", 0, 0, dev()).wait_recv()

    @pl.when(y_rel == 1)
    def _():
        dsend[y_odd, 0:HF, :] = (dwf[y_odd, 0:HF, :] + yh[...].astype(F32)).astype(BF)
        rcopy(dsend.at[y_odd, rows_a4], yf.at[0, rows_a4], "ys", 0, 0, dev(yy=yp)).start()

    @pl.when(y_rel == 3)
    def _():
        dsend[y_odd, HF:F, :] = (dwf[y_odd, HF:F, :] + yh[...].astype(F32)).astype(BF)
        rcopy(dsend.at[y_odd, rows_b4], yf.at[1, rows_b4], "ys", 3, 3, dev(yy=ym)).start()

    rcopy(pss.at[0, rows_b], xf.at[0, rows_b], "xs", 0, 0, dev()).wait_recv()
    rcopy(pss.at[0, rows_a], xf.at[0, rows_a], "xs", 2, 2, dev()).wait_recv()
    rcopy(pss.at[1, rows_a], xf.at[1, rows_a], "xs", 1, 1, dev()).wait_recv()
    rcopy(pss.at[1, rows_b], xf.at[1, rows_b], "xs", 3, 3, dev()).wait_recv()
    gio[...] = (loc[...] + xf[0].astype(F32) + xf[1].astype(F32)).astype(BF)
    out_gi = pltpu.make_async_copy(gio, gi_hbm.at[0], ls.at[5])
    out_gi.start()

    @pl.when(y_own)
    def _():
        for i, rows in ((0, rows_a4), (1, rows_b4)):
            for side in range(2):
                rcopy(
                    dsend.at[0, rows], yf.at[side, rows], "ys", 2 * side + i, 2 * side + i, dev()
                ).wait_recv()
        dwf[par_y] = dwf[par_y] + yf[0].astype(F32) + yf[1].astype(F32)

        def rows_for(to):
            return pl.ds(pl.multiple_of(to * ZR, 16), ZR)

        started = []

        def hop(name, send, got, step, to, n, way, cut):
            at, width = CUTS[cut]
            span = pl.ds(at, width)
            value = dwf[par_y, rows_for(to), span]
            if step > 0:
                idx = 2 * (step - 1) + cut
                rcopy(send.at[step - 1, :, span], got.at[step - 1, :, span], name, idx, idx, dev()).wait_recv()
                value = value + got[step - 1, :, span].astype(F32)
            if step == n:
                return value
            send[step, :, span] = value.astype(BF)
            idx = 2 * step + cut
            copy = rcopy(send.at[step, :, span], got.at[step, :, span], name, idx, idx, dev(zz=way))
            copy.start()
            started.append(copy)

        for step in range(4):
            for cut in range(2):
                hop("zp", zps, zpr, step, lax.rem(z + 4 - step, NZ), 4, zp, cut)
                if step < 3:
                    hop("zm", zms, zmr, step, lax.rem(z + 5 + step, NZ), 3, zm, cut)
        for cut in range(2):
            at, width = CUTS[cut]
            span = pl.ds(at, width)
            value = hop("zp", zps, zpr, 4, z, 4, zp, cut)
            idx = 4 + cut
            rcopy(zms.at[2, :, span], zmr.at[2, :, span], "zm", idx, idx, dev()).wait_recv()
            fin[:, span] = weight_scale * (value + zmr[2, :, span].astype(F32))
        keep = pl.ds(pl.multiple_of(c * OUT, 8), OUT)
        give = pl.ds(pl.multiple_of(other * OUT, 8), OUT)
        copy = rcopy(fin.at[give], gwv, "fp", 0, 0, dev(cc=other))
        copy.start()
        started.append(copy)
        out = pltpu.make_async_copy(fin.at[keep], gw_hbm, ls.at[6])
        out.start()
        for copy in started:
            copy.wait_send()
        out.wait()

    @pl.when(jnp.logical_not(y_own))
    def _():
        rcopy(fin.at[pl.ds(0, OUT)], gwv, "fp", 0, 0, dev()).wait_recv()
        out = pltpu.make_async_copy(gwv, gw_hbm, ls.at[6])
        out.start()
        rcopy(dsend.at[par_y, rows_a4], yh, "yh", 0, 0, dev()).wait_send()
        rcopy(dsend.at[par_y, rows_b4], yh, "yh", 1, 0, dev()).wait_send()
        out.wait()

    out_gi.wait()
    to_p.wait_send()
    to_m.wait_send()

    @pl.when(jnp.logical_not(x_own))
    def _():
        to_other.wait_send()

    @pl.when(x_rel == 1)
    def _():
        pass_a.wait_send()

    @pl.when(x_rel == 3)
    def _():
        pass_b.wait_send()

    @pl.when(y_rel == 1)
    def _():
        rcopy(dsend.at[y_odd, rows_a4], yf.at[0, rows_a4], "ys", 0, 0, dev()).wait_send()
        rcopy(dsend.at[y_odd, rows_b4], yf.at[0, rows_b4], "ys", 1, 1, dev()).wait_send()

    @pl.when(y_rel == 3)
    def _():
        rcopy(dsend.at[y_odd, rows_a4], yf.at[1, rows_a4], "ys", 2, 2, dev()).wait_send()
        rcopy(dsend.at[y_odd, rows_b4], yf.at[1, rows_b4], "ys", 3, 3, dev()).wait_send()

    for copy in sent_dz + sent_a1 + sent_yx + sent_a2 + [sent_vg] + sent_x:
        copy.wait_send()


def local(inputs, value_weight, cotangent, spikes_q, spikes_k, log_decay):
    grad_scale = 1.0 / (2.25 * E * math.sqrt(T * NY * NZ))
    weight_scale = 1.0 / math.sqrt(2 * T * NY * NZ)
    vm = pltpu.VMEM
    anywhere = pl.BlockSpec(memory_space=pl.ANY)

    def body(*refs):
        kernel(grad_scale, weight_scale, *refs)

    return pl.pallas_call(
        body,
        out_shape=(
            jax.ShapeDtypeStruct((1, T, F), BF),
            jax.ShapeDtypeStruct((OUT, F), F32),
        ),
        in_specs=[anywhere] * 5 + [pl.BlockSpec(memory_space=pltpu.VMEM)],
        out_specs=(anywhere, anywhere),
        scratch_shapes=[
            vm((NX * F, F), BF),
            vm((T, F), BF),
            vm((T, F), jnp.int32),
            vm((T, F), jnp.int32),
            vm((2, 2, T, F), BF),
            vm((E, T), F32),
            vm((T, E), F32),
            vm((8, E), F32),
            vm((NZ, 8, E), F32),
            vm((NZ, H, SL, E), BF),
            vm((NZ, H, SL, E), BF),
            vm((NZ, H, SL, E), F32),
            vm((YROWS, E), F32),
            vm((NY, YROWS, E), F32),
            vm((NZ, H, SL, E), BF),
            vm((NZ, H, SL, E), BF),
            vm((T, F), F32),
            vm((2, T, F), BF),
            vm((T, F), BF),
            vm((2, T, F), BF),
            vm((2, HT, F), F32),
            vm((2, HT, F), BF),
            vm((2, T, F), BF),
            vm((T, F), BF),
            vm((2, F, F), F32),
            vm((2, F, F), BF),
            vm((HF, F), BF),
            vm((2, F, F), BF),
            vm((4, ZR, F), BF),
            vm((4, ZR, F), BF),
            vm((3, ZR, F), BF),
            vm((3, ZR, F), BF),
            vm((ZR, F), F32),
            vm((OUT, F), F32),
            pltpu.SemaphoreType.DMA((NSEM,)),
            pltpu.SemaphoreType.DMA((NSEM,)),
            pltpu.SemaphoreType.DMA((7,)),
        ],
        compiler_params=pltpu.CompilerParams(
            collective_id=0, has_side_effects=True, vmem_limit_bytes=60 * 1024 * 1024
        ),
    )(inputs, value_weight, cotangent, spikes_q, spikes_k, log_decay)


def solution(mesh):
    return jax.shard_map(
        local,
        mesh=mesh,
        in_specs=(
            P("dp", "seq", "head"),
            P(None, "head"),
            P("dp", "seq", "head"),
            P("dp", "seq", "head"),
            P("dp", "seq", "head"),
            P("dp", "head", "seq"),
        ),
        out_specs=(P("dp", "seq", "head"), P(("seq", "dp"), "head")),
        check_vma=False,
    )
```

time: 512 us -> 109 us (0.21)
  waiting for transfers between devices: 337 us -> 0 us
  Pallas kernels: 0 us -> 104 us
  blocking collectives: 64.4 us -> 0 us
  other arithmetic: 50.1 us -> 0 us
  matrix products: 28.2 us -> 0 us
  between operations: 15.2 us -> 0.65 us
  local copies, waits for them, and re-layouts: 10.6 us -> 4.22 us
    unnamed x5 -> x0, waiting for transfers between devices: 206 us -> none
    pallas_call x0 -> x1, Pallas kernels: none -> 104 us  [local(): pl.pallas_call(body, out_shape=(jax.ShapeDtypeStruct((1, T, F), BF), jax....]
    reduce_scatter x1 -> x0, waiting for transfers between devices: 73.6 us -> none  [local(): lax.psum_scatter(input_term, 'head', scatter_dimension=1, tiled=True)]
    unnamed x1 -> x0, blocking collectives: 64.4 us -> none
    all_gather x2 -> x0, waiting for transfers between devices: 57.9 us -> none  [the longest x1 54.8 us: carried_in(): everything = jax.tree.map(lambda part: lax.all_gather(part, axis), array)]
    select_n x32 -> x0, other arithmetic: 36.8 us -> none  [lap(): return jax.tree.map(lambda a, b: jnp.where(reached, a, b), new, before)]
    dot_general x5 -> x0, matrix products: 28.2 us -> none  [the longest x1 8.95 us: local(): lax.dot_general(value_grad, value_weight, (((1,), (1,)), ((), ())), prefe...]
    convert_element_type x2 -> x0, other arithmetic: 5.33 us -> none  [the longest x1 3.45 us: local(): query_f32 = spikes_q.reshape(shape_four).astype(jnp.float32)]
  transfers between devices with their start and end apart: 4 -> 0, of which waited for: 4 -> 0; matrix products, arithmetic and copies ran while one was open for 12% -> 0% of each run, Pallas kernels for 0% -> 0%
where the time goes in v1:
time: 109 us
  Pallas kernels  104 us (95%)
  local copies, waits for them, and re-layouts  4.22 us (4%)
    pallas_call x1, Pallas kernels, local(): pl.pallas_call(body, out_shape=(jax.ShapeDtypeStruct((1, T, F), BF), jax....  104 us
    unnamed x5, local copies, waits for them, and re-layouts  4.22 us

profile of v1, /device:TPU:5, one launch (start us, length us, event | category | flops | bytes accessed | tf_op | source)
XLA Modules:
  0.0 109.1 jit_solution(8378515668728807596)
XLA Ops:
  0.6 1.3 %copy.8.refs_5_ = f32[1,7,512]{2,1,0:T(8,128)} copy(f32[1,7,512]{2,0,1:T(1,128)} %param.11) | data formatting | bytes 28672 | tf_op args[5]
  1.9 104.2 %shard_map.77 = (bf16[1,512,896]{2,1,0:T(8,128)(2,1)}, f32[56,896]{1,0:T(8,128)}) custom-call(bf16[1,512,896]{2,1,0:T(8,128)(2,1)} %refs_0_.1, bf16[3584,896]{1,0:T(8,128)(2,1)} %refs_1_.1, bf16[1,512,896]{2,1,0:T(8,128)(2,1)} %refs_2_.1, s32[1,512,896]{2,1,0:T(8,128)} %refs_3_.1, s32[1,512,896]{2,1,0:T(8,128)} %refs_4_.1, f32[1,7,512]{2,1,0:T(8,128)} %copy.8.refs_5_), custom_call_target="tpu_custom_call" | custom-call | tf_op jit(solution)/shard_map/pallas_call | solution.py:447
  106.1 0.0 copy-start
  106.2 2.2 %copy.11 = bf16[1,512,896]{2,1,0:T(8,128)(2,1)} copy(bf16[1,512,896]{2,1,0:T(8,128)(2,1)} %get-tuple-element.4) | data formatting | bytes 1835008
  108.4 0.0 copy-done
  108.4 0.7 copy.12
Async XLA Ops:
  106.1 2.2 %copy-start = (f32[56,896]{1,0:T(8,128)S(1)}, f32[56,896]{1,0:T(8,128)}, u32[]{:S(2)}) copy-start(f32[56,896]{1,0:T(8,128)} %get-tuple-element.5) | copy-start | bytes 602116

commit v2 on v1

--- a/solution.py
+++ b/solution.py
@@ -15,7 +15,8 @@
 OUT = ZR // 2
 SL = E // NZ
 YROWS = H * SL + 8
-CUTS = ((0, 512), (512, 384))
+CUTS = ((0, 384), (384, 256), (640, 256))
+NC = len(CUTS)
 BF, F32 = jnp.bfloat16, jnp.float32
 MESH = pl.DeviceIdType.MESH
 
@@ -23,7 +24,7 @@
 _count = 0
 for _name, _n in (
     ("dz", 8), ("a1", 8), ("a2", 8), ("yx", 4), ("xd", 2), ("xp", 1), ("xf", 2), ("vg", 1),
-    ("xh", 2), ("xs", 4), ("yh", 2), ("ys", 4), ("zp", 8), ("zm", 6), ("fp", 1),
+    ("xh", 2), ("xs", 4), ("yh", 2 * NC), ("ys", 4 * NC), ("zp", 4 * NC), ("zm", 3 * NC), ("fp", 1),
 ):
     _names[_name] = _count
     _count += _n
@@ -36,9 +37,9 @@
 
 def kernel(
     grad_scale, weight_scale,
-    x_hbm, w_hbm, g_hbm, q_hbm, k_hbm, ld_ref,
+    x_hbm, w_hbm, g_hbm, q_hbm, k_hbm, ld_hbm,
     gi_hbm, gw_hbm,
-    wv, gv, qv, kv, xg, cumr, cumc, dzs, dzr, tsend, trecv, lbuf, ysend, yrecv, csend, crecv,
+    ldv, wv, gv, qv, kv, xg, cumr, cumc, dzs, dzr, tsend, trecv, lbuf, ysend, yrecv, csend, crecv,
     loc, vgs, p2s, pss, pf, xh, xf, gio, dwf, dsend, yh, yf, zps, zpr, zms, zmr, fin, gwv,
     ss, rs, ls,
 ):
@@ -70,6 +71,7 @@
         pltpu.make_async_copy(g_hbm.at[0], gv, ls.at[1]),
         pltpu.make_async_copy(k_hbm.at[0], kv, ls.at[2]),
         pltpu.make_async_copy(w_hbm, wv, ls.at[3]),
+        pltpu.make_async_copy(ld_hbm, ldv, ls.at[7]),
     ]
     for load in loads:
         load.start()
@@ -105,7 +107,8 @@
         lax.broadcasted_iota(jnp.int32, (T, T), 0) <= lax.broadcasted_iota(jnp.int32, (T, T), 1)
     ).astype(F32).astype(BF)
     cumr[...] = jnp.zeros_like(cumr)
-    cumr[0:H, :] = ld_ref[0]
+    loads[4].wait()
+    cumr[0:H, :] = ldv[0]
     rest = cumr[...]
     total = jnp.zeros((E, T), F32)
     for _ in range(3):
@@ -274,41 +277,77 @@
     y_odd = 1 - par_y
     y_rel = lax.rem(2 * c + y_odd - y + NY, NY)
 
-    @pl.when(x_own)
-    def _():
-        own_in.wait()
-        rcopy(x_hbm.at[0], xg.at[par_x, other], "xp", 0, 0, dev()).wait_recv()
-
-    @pl.when(jnp.logical_not(x_own))
-    def _():
-        far_a, far_b = xg.at[par_x, :, rows_a, :], xg.at[par_x, :, rows_b, :]
-        rcopy(far_a, far_a, "xf", 0, 0, dev()).wait_recv()
-        rcopy(far_b, far_b, "xf", 1, 1, dev()).wait_recv()
-
     rcopy(vgs.at[other], vgs.at[other], "vg", 0, 0, dev()).wait_recv()
+    rows_a4, rows_b4 = pl.ds(0, HF), pl.ds(HF, HF)
+    spans = [pl.ds(at, width) for at, width in CUTS]
+
+    def to_near(slot, cut):
+        half = rows_a4, rows_b4
+        return [
+            rcopy(dsend.at[slot, half[i], spans[cut]], yh.at[:, spans[cut]], "yh", i * NC + cut, cut,
+                  dev(yy=(yp, ym)[i]))
+            for i in range(2)
+        ]
+
+    def to_owner(slot, side, half, cut):
+        rows = (rows_a4, rows_b4)[half]
+        idx = (2 * side + half) * NC + cut
+        return rcopy(
+            dsend.at[slot, rows, spans[cut]], yf.at[side, rows, spans[cut]], "ys", idx, idx,
+            dev(yy=(yp, ym)[side]),
+        )
 
     def weight_of(i, carry):
-        slot = lax.rem(par_y + jnp.where(y_own, 1, 0) + i, 2)
+        slot = lax.rem(par_x + jnp.where(x_own, 0, 1) + i, 2)
+
+        @pl.when(jnp.logical_and(slot == par_x, x_own))
+        def _():
+            own_in.wait()
+            rcopy(x_hbm.at[0], xg.at[par_x, other], "xp", 0, 0, dev()).wait_recv()
+
+        @pl.when(jnp.logical_and(slot == par_x, jnp.logical_not(x_own)))
+        def _():
+            far_a, far_b = xg.at[par_x, :, rows_a, :], xg.at[par_x, :, rows_b, :]
+            rcopy(far_a, far_a, "xf", 0, 0, dev()).wait_recv()
+            rcopy(far_b, far_b, "xf", 1, 1, dev()).wait_recv()
+
         dwf[slot] = dot(xg[slot].reshape(2 * T, F), vgs[...].reshape(2 * T, F), 0, 0)
         dsend[slot] = dwf[slot].astype(BF)
-        first_a, first_b = pl.ds(0, HF), pl.ds(HF, HF)
 
         @pl.when(jnp.logical_and(slot == par_y, jnp.logical_not(y_own)))
         def _():
-            rcopy(dsend.at[slot, first_a], yh, "yh", 0, 0, dev(yy=yp)).start()
-            rcopy(dsend.at[slot, first_b], yh, "yh", 1, 0, dev(yy=ym)).start()
+            for cut in range(NC):
+                for copy in to_near(slot, cut):
+                    copy.start()
 
         @pl.when(jnp.logical_and(slot == y_odd, y_rel == 1))
         def _():
-            rcopy(dsend.at[slot, first_b], yf.at[0, first_b], "ys", 1, 1, dev(yy=yp)).start()
+            for cut in range(NC):
+                to_owner(slot, 0, 1, cut).start()
 
         @pl.when(jnp.logical_and(slot == y_odd, y_rel == 3))
         def _():
-            rcopy(dsend.at[slot, first_a], yf.at[1, first_a], "ys", 2, 2, dev(yy=ym)).start()
+            for cut in range(NC):
+                to_owner(slot, 1, 0, cut).start()
 
         return carry
 
     lax.fori_loop(0, 2, weight_of, 0)
+    loc[...] = product(x)
+
+    for cut in range(NC):
+        span = spans[cut]
+        rcopy(dsend.at[0, rows_a4, span], yh.at[:, span], "yh", cut, cut, dev()).wait_recv()
+
+        @pl.when(y_rel == 1)
+        def _():
+            dsend[y_odd, 0:HF, span] = (dwf[y_odd, 0:HF, span] + yh[:, span].astype(F32)).astype(BF)
+            to_owner(y_odd, 0, 0, cut).start()
+
+        @pl.when(y_rel == 3)
+        def _():
+            dsend[y_odd, HF:F, span] = (dwf[y_odd, HF:F, span] + yh[:, span].astype(F32)).astype(BF)
+            to_owner(y_odd, 1, 1, cut).start()
 
     rcopy(p2s.at[rows_a], xh.at[0], "xh", 0, 0, dev()).wait_recv()
     pss[0, :HT, :] = (pf[0] + xh[0].astype(F32)).astype(BF)
@@ -320,20 +359,52 @@
     copy = rcopy(pss.at[1, rows_b], xf.at[1, rows_b], "xs", 3, 3, dev(xx=xm))
     copy.start()
     sent_x.append(copy)
-    loc[...] = product(x)
-
-    rows_a4, rows_b4 = pl.ds(0, HF), pl.ds(HF, HF)
-    rcopy(dsend.at[0, rows_a4], yh, "yh", 0, 0, dev()).wait_recv()
-
-    @pl.when(y_rel == 1)
-    def _():
-        dsend[y_odd, 0:HF, :] = (dwf[y_odd, 0:HF, :] + yh[...].astype(F32)).astype(BF)
-        rcopy(dsend.at[y_odd, rows_a4], yf.at[0, rows_a4], "ys", 0, 0, dev(yy=yp)).start()
-
-    @pl.when(y_rel == 3)
-    def _():
-        dsend[y_odd, HF:F, :] = (dwf[y_odd, HF:F, :] + yh[...].astype(F32)).astype(BF)
-        rcopy(dsend.at[y_odd, rows_b4], yf.at[1, rows_b4], "ys", 3, 3, dev(yy=ym)).start()
+
+    keep = pl.ds(pl.multiple_of(c * OUT, 8), OUT)
+    give = pl.ds(pl.multiple_of(other * OUT, 8), OUT)
+    out_fin = pltpu.make_async_copy(fin.at[keep], gw_hbm, ls.at[6])
+    give_fin = rcopy(fin.at[give], gwv, "fp", 0, 0, dev(cc=other))
+
+    def along_z(name, step, cut):
+        send, got, way = (zps, zpr, zp) if name == "zp" else (zms, zmr, zm)
+        idx = step * NC + cut
+        part = (step, slice(None), spans[cut])
+        return rcopy(send.at[part], got.at[part], name, idx, idx, dev(zz=way))
+
+    def hop(name, step, to, cut, last):
+        send, got = (zps, zpr) if name == "zp" else (zms, zmr)
+        span = spans[cut]
+        value = dwf[par_y, pl.ds(pl.multiple_of(to * ZR, 16), ZR), span]
+        if step > 0:
+            along_z(name, step - 1, cut).wait_recv()
+            value = value + got[step - 1, :, span].astype(F32)
+        if step == last:
+            return value
+        send[step, :, span] = value.astype(BF)
+        along_z(name, step, cut).start()
+
+    @pl.when(y_own)
+    def _():
+        for tick in range(4 + NC):
+            for cut in range(NC):
+                step, span = tick - cut, spans[cut]
+                if step < 0 or step > 4:
+                    continue
+                if step == 0:
+                    for side in range(2):
+                        for half in range(2):
+                            to_owner(0, side, half, cut).wait_recv()
+                    dwf[par_y, :, span] = (
+                        dwf[par_y, :, span] + yf[0, :, span].astype(F32) + yf[1, :, span].astype(F32)
+                    )
+                value = hop("zp", step, lax.rem(z + 4 - step + NZ, NZ), cut, 4)
+                if step < 3:
+                    hop("zm", step, lax.rem(z + 5 + step, NZ), cut, 3)
+                if step == 4:
+                    along_z("zm", 2, cut).wait_recv()
+                    fin[:, span] = weight_scale * (value + zmr[2, :, span].astype(F32))
+        give_fin.start()
+        out_fin.start()
 
     rcopy(pss.at[0, rows_b], xf.at[0, rows_b], "xs", 0, 0, dev()).wait_recv()
     rcopy(pss.at[0, rows_a], xf.at[0, rows_a], "xs", 2, 2, dev()).wait_recv()
@@ -345,64 +416,22 @@
 
     @pl.when(y_own)
     def _():
-        for i, rows in ((0, rows_a4), (1, rows_b4)):
-            for side in range(2):
-                rcopy(
-                    dsend.at[0, rows], yf.at[side, rows], "ys", 2 * side + i, 2 * side + i, dev()
-                ).wait_recv()
-        dwf[par_y] = dwf[par_y] + yf[0].astype(F32) + yf[1].astype(F32)
-
-        def rows_for(to):
-            return pl.ds(pl.multiple_of(to * ZR, 16), ZR)
-
-        started = []
-
-        def hop(name, send, got, step, to, n, way, cut):
-            at, width = CUTS[cut]
-            span = pl.ds(at, width)
-            value = dwf[par_y, rows_for(to), span]
-            if step > 0:
-                idx = 2 * (step - 1) + cut
-                rcopy(send.at[step - 1, :, span], got.at[step - 1, :, span], name, idx, idx, dev()).wait_recv()
-                value = value + got[step - 1, :, span].astype(F32)
-            if step == n:
-                return value
-            send[step, :, span] = value.astype(BF)
-            idx = 2 * step + cut
-            copy = rcopy(send.at[step, :, span], got.at[step, :, span], name, idx, idx, dev(zz=way))
-            copy.start()
-            started.append(copy)
-
-        for step in range(4):
-            for cut in range(2):
-                hop("zp", zps, zpr, step, lax.rem(z + 4 - step, NZ), 4, zp, cut)
-                if step < 3:
-                    hop("zm", zms, zmr, step, lax.rem(z + 5 + step, NZ), 3, zm, cut)
-        for cut in range(2):
-            at, width = CUTS[cut]
-            span = pl.ds(at, width)
-            value = hop("zp", zps, zpr, 4, z, 4, zp, cut)
-            idx = 4 + cut
-            rcopy(zms.at[2, :, span], zmr.at[2, :, span], "zm", idx, idx, dev()).wait_recv()
-            fin[:, span] = weight_scale * (value + zmr[2, :, span].astype(F32))
-        keep = pl.ds(pl.multiple_of(c * OUT, 8), OUT)
-        give = pl.ds(pl.multiple_of(other * OUT, 8), OUT)
-        copy = rcopy(fin.at[give], gwv, "fp", 0, 0, dev(cc=other))
-        copy.start()
-        started.append(copy)
-        out = pltpu.make_async_copy(fin.at[keep], gw_hbm, ls.at[6])
-        out.start()
-        for copy in started:
-            copy.wait_send()
-        out.wait()
+        for cut in range(NC):
+            for step in range(4):
+                along_z("zp", step, cut).wait_send()
+            for step in range(3):
+                along_z("zm", step, cut).wait_send()
+        give_fin.wait_send()
+        out_fin.wait()
 
     @pl.when(jnp.logical_not(y_own))
     def _():
         rcopy(fin.at[pl.ds(0, OUT)], gwv, "fp", 0, 0, dev()).wait_recv()
         out = pltpu.make_async_copy(gwv, gw_hbm, ls.at[6])
         out.start()
-        rcopy(dsend.at[par_y, rows_a4], yh, "yh", 0, 0, dev()).wait_send()
-        rcopy(dsend.at[par_y, rows_b4], yh, "yh", 1, 0, dev()).wait_send()
+        for cut in range(NC):
+            for copy in to_near(par_y, cut):
+                copy.wait_send()
         out.wait()
 
     out_gi.wait()
@@ -421,15 +450,12 @@
     def _():
         pass_b.wait_send()
 
-    @pl.when(y_rel == 1)
-    def _():
-        rcopy(dsend.at[y_odd, rows_a4], yf.at[0, rows_a4], "ys", 0, 0, dev()).wait_send()
-        rcopy(dsend.at[y_odd, rows_b4], yf.at[0, rows_b4], "ys", 1, 1, dev()).wait_send()
-
-    @pl.when(y_rel == 3)
-    def _():
-        rcopy(dsend.at[y_odd, rows_a4], yf.at[1, rows_a4], "ys", 2, 2, dev()).wait_send()
-        rcopy(dsend.at[y_odd, rows_b4], yf.at[1, rows_b4], "ys", 3, 3, dev()).wait_send()
+    for side in range(2):
+        @pl.when(y_rel == 1 + 2 * side)
+        def _():
+            for half in range(2):
+                for cut in range(NC):
+                    to_owner(y_odd, side, half, cut).wait_send()
 
     for copy in sent_dz + sent_a1 + sent_yx + sent_a2 + [sent_vg] + sent_x:
         copy.wait_send()
@@ -450,9 +476,10 @@
             jax.ShapeDtypeStruct((1, T, F), BF),
             jax.ShapeDtypeStruct((OUT, F), F32),
         ),
-        in_specs=[anywhere] * 5 + [pl.BlockSpec(memory_space=pltpu.VMEM)],
+        in_specs=[anywhere] * 6,
         out_specs=(anywhere, anywhere),
         scratch_shapes=[
+            vm((1, H, T), F32),
             vm((NX * F, F), BF),
             vm((T, F), BF),
             vm((T, F), jnp.int32),
@@ -489,7 +516,7 @@
             vm((OUT, F), F32),
             pltpu.SemaphoreType.DMA((NSEM,)),
             pltpu.SemaphoreType.DMA((NSEM,)),
-            pltpu.SemaphoreType.DMA((7,)),
+            pltpu.SemaphoreType.DMA((8,)),
         ],
         compiler_params=pltpu.CompilerParams(
             collective_id=0, has_side_effects=True, vmem_limit_bytes=60 * 1024 * 1024

time: 109 us -> 101 us (0.927)
  Pallas kernels: 104 us -> 95.5 us
    pallas_call x1, Pallas kernels: 104 us -> 95.5 us  [local(): pl.pallas_call(body, out_shape=(jax.ShapeDtypeStruct((1, T, F), BF), jax....]
where the time goes in v2:
time: 101 us; the launch traced here: 100 us
  Pallas kernels  95.5 us (95%)
  local copies, waits for them, and re-layouts  4.22 us (4%)
    pallas_call x1, Pallas kernels, local(): pl.pallas_call(body, out_shape=(jax.ShapeDtypeStruct((1, T, F), BF), jax....  95.5 us
    unnamed x5, local copies, waits for them, and re-layouts  4.22 us

profile of v2, /device:TPU:5, one launch (start us, length us, event | category | flops | bytes accessed | tf_op | source)
XLA Modules:
  0.0 100.4 jit_solution(4395119777429464995)
XLA Ops:
  0.6 1.3 %copy.8.refs_5_ = f32[1,7,512]{2,1,0:T(8,128)} copy(f32[1,7,512]{2,0,1:T(1,128)} %param.11) | data formatting | bytes 28672 | tf_op args[5]
  1.9 95.5 %shard_map.77 = (bf16[1,512,896]{2,1,0:T(8,128)(2,1)}, f32[56,896]{1,0:T(8,128)}) custom-call(bf16[1,512,896]{2,1,0:T(8,128)(2,1)} %refs_0_.1, bf16[3584,896]{1,0:T(8,128)(2,1)} %refs_1_.1, bf16[1,512,896]{2,1,0:T(8,128)(2,1)} %refs_2_.1, s32[1,512,896]{2,1,0:T(8,128)} %refs_3_.1, s32[1,512,896]{2,1,0:T(8,128)} %refs_4_.1, f32[1,7,512]{2,1,0:T(8,128)} %copy.8.refs_5_), custom_call_target="tpu_custom_call" | custom-call | tf_op jit(solution)/shard_map/pallas_call | solution.py:473
  97.5 0.0 copy-start
  97.5 2.2 %copy.11 = bf16[1,512,896]{2,1,0:T(8,128)(2,1)} copy(bf16[1,512,896]{2,1,0:T(8,128)(2,1)} %get-tuple-element.4) | data formatting | bytes 1835008
  99.7 0.0 copy-done
  99.7 0.7 copy.12
Async XLA Ops:
  97.5 2.2 %copy-start = (f32[56,896]{1,0:T(8,128)S(1)}, f32[56,896]{1,0:T(8,128)}, u32[]{:S(2)}) copy-start(f32[56,896]{1,0:T(8,128)} %get-tuple-element.5) | copy-start | bytes 602116
